TPU v7x, 32 devices: a whole 2x2x4 slice. The times are simulated.
32 devices in a mesh: groups: 2 (over x), seq: 16 (over z, y, core).
Axes of the slice: x: 2, y: 2, z: 4, core: 2. Of those that a mesh axis runs over, the one named last changes fastest.
Arguments:
- cache_keys: bfloat16 [131072, 1024], P(('groups', 'seq')), parts along dimension 0, may hold values from -48 to 48
- cache_values: bfloat16 [131072, 1024], P(('groups', 'seq')), parts along dimension 0, may hold values from -6 to 6
- sketch_matrix: float32 [1024, 160], replicated, may hold values from -6 to 6
- queries: bfloat16 [6, 8192], P('groups'), parts along dimension 0, may hold values from -2000 to 2000
- fresh_keys: bfloat16 [6, 1024], P('groups'), parts along dimension 0, may hold values from -20 to 20
- fresh_values: bfloat16 [6, 1024], P('groups'), parts along dimension 0, may hold values from -6 to 6
- chosen: int32 [6, 8, 256], P('groups'), parts along dimension 0, may hold values from 0 to 8191, as said below
- shard_counts: int32 [6, 8, 16], P('groups'), parts along dimension 0, may hold values from 0 to 48, as said below
- outliers: int32 [64], P('groups'), parts along dimension 0, may hold values from 0 to 8191, as said below
Outputs:
- attended: bfloat16 [6, 8192], P('groups', 'seq'), parts along dimension 0
- key_factor: float32 [131072, 160], P(('groups', 'seq')), parts along dimension 0
There are 2 independent parts, one for each index of `groups`. A program takes and returns all parts, laid end to end along the dimension named above; an argument that names none is the same for every part. Nothing has to cross between parts.
Inputs may be any that keep to these rules, and one draw needn't show every extreme that they name: Each list chosen[t, g] holds distinct span numbers in ascending order, none of them an outlier span; shard s holds spans s * 512 to (s+1) * 512 - 1. shard_counts[t, g, s] is the number of entries of chosen[t, g] on shard s; they sum to 256; the most is 48, reached in every list. `outliers`: distinct span numbers in ascending order; at most 4 on one shard, reached on some shard.
All inputs are finite; a program needn't handle non-finite values.
Results may differ from a plain program's by a relative error of at most 0.0228.
Values may be sent and summed in bfloat16 or wider, within the bound.
A program may use at most 128 MiB of HBM per device.

v0:
```python
import jax
import jax.numpy as jnp
from jax import lax
from jax.sharding import PartitionSpec as P

KVH = 8
HD = 128
QH = 64
SPAN = 8
OMOST = 4


def merged_2(x, axis, combine):
    everything = jax.tree.map(lambda part: lax.all_gather(part, axis), x)
    leading = jax.tree.map(lambda part: part[0], everything)

    def step(k, so_far):
        return combine(so_far, jax.tree.map(lambda part: part[k], everything))

    return lax.fori_loop(1, lax.axis_size(axis), step, leading)


def rotate(vectors, positions):
    half_width = vectors.shape[-1] // 2
    exponents = jnp.arange(half_width, dtype=jnp.float32) * (2.0 / vectors.shape[-1])
    inverse_freq = jnp.exp(-jnp.log(jnp.float32(500000.0)) * exponents)
    angles = positions.astype(jnp.float32)[..., None] * inverse_freq
    cosine = jnp.cos(angles)
    sine = jnp.sin(angles)
    first_half = vectors[..., :half_width]
    second_half = vectors[..., half_width:]
    return jnp.concatenate(
        [first_half * cosine - second_half * sine, second_half * cosine + first_half * sine],
        axis=-1,
    )


def make_basis(sketch):
    small_gram = jnp.dot(sketch.T, sketch, precision=lax.Precision.HIGHEST)
    lower = jnp.linalg.cholesky(small_gram)
    solved = lax.linalg.triangular_solve(lower, sketch.T, left_side=True, lower=True)
    return solved.T.astype(jnp.bfloat16)


def softmax_part(query_rows, key_rows, value_rows, is_live):
    score_scale = 1.0 / jnp.sqrt(jnp.float32(query_rows.shape[-1]))
    scores = (
        jnp.einsum(
            "...qd,...ld->...ql",
            query_rows,
            key_rows.astype(jnp.float32),
            precision=lax.Precision.HIGHEST,
        )
        * score_scale
    )
    live_mask = is_live[..., None, :]
    scores = jnp.where(live_mask, scores, -1e30)
    run_max = jnp.max(scores, axis=-1)
    weights = jnp.exp(scores - run_max[..., None]) * live_mask
    run_sum = jnp.sum(weights, axis=-1)
    run_out = jnp.einsum(
        "...ql,...ld->...qd",
        weights,
        value_rows.astype(jnp.float32),
        precision=lax.Precision.HIGHEST,
    )
    return (run_max, run_sum, run_out)


def combine(earlier, later):
    joint_max = jnp.maximum(earlier[0], later[0])
    scale_early = jnp.exp(earlier[0] - joint_max)
    scale_late = jnp.exp(later[0] - joint_max)
    return (
        joint_max,
        earlier[1] * scale_early + later[1] * scale_late,
        earlier[2] * scale_early[..., None] + later[2] * scale_late[..., None],
    )


def on_device(
    cache_keys,
    cache_values,
    sketch_matrix,
    queries,
    fresh_keys,
    fresh_values,
    chosen,
    shard_counts,
    outliers,
):
    seq_len, feature_width = cache_keys.shape
    devices = lax.axis_size("seq")
    myself = lax.axis_index("seq")
    length = seq_len * devices
    steps = queries.shape[0]
    group_size = QH // KVH
    per_device = QH // devices
    contract = (((0,), (0,)), ((), ()))
    gram_share = (
        lax.psum_scatter(
            lax.dot_general(cache_keys, cache_keys, contract, preferred_element_type=jnp.float32),
            "seq",
            scatter_dimension=0,
            tiled=True,
        )
        / length
    )
    sketch_share = jnp.dot(gram_share, sketch_matrix, precision=lax.Precision.HIGHEST)
    sketch = lax.all_gather(sketch_share, "seq", axis=0, tiled=True)
    key_basis = make_basis(sketch)
    rank_width = key_basis.shape[1]
    key_factor = jnp.dot(cache_keys, key_basis, preferred_element_type=jnp.float32)
    spans_dev = seq_len // SPAN
    most_slots = 3 * chosen.shape[2] // devices
    preceding = jnp.cumsum(shard_counts, axis=2) - shard_counts
    list_start = lax.dynamic_index_in_dim(preceding, myself, 2, keepdims=False)
    own_count = lax.dynamic_index_in_dim(shard_counts, myself, 2, keepdims=False)
    padded_list = jnp.concatenate([chosen, jnp.zeros((steps, KVH, most_slots), jnp.int32)], axis=2)
    slot_ids = jnp.arange(most_slots, dtype=jnp.int32)
    picked = jnp.take_along_axis(padded_list, list_start[..., None] + slot_ids, axis=2)
    is_live = slot_ids < own_count[..., None]
    shard_base = myself * spans_dev
    local_span = jnp.clip(picked - shard_base, 0, spans_dev - 1)
    factor_spans = key_factor.reshape(spans_dev, SPAN, rank_width)[local_span]
    basis_heads = key_basis.reshape(KVH, HD, rank_width).astype(jnp.float32)
    rebuilt = jnp.einsum(
        "tgmcr,gdr->tgmcd", factor_spans, basis_heads, precision=lax.Precision.HIGHEST
    )
    token_pos = (local_span + shard_base)[..., None] * SPAN + jnp.arange(SPAN, dtype=jnp.int32)
    sel_keys = rotate(rebuilt, token_pos).astype(jnp.bfloat16)
    value_blocks = cache_values.reshape(spans_dev, SPAN, KVH, HD)
    head_ids = jnp.arange(KVH, dtype=jnp.int32)
    sel_values = value_blocks[local_span, :, head_ids[None, :, None], :]
    outlier_here = outliers // spans_dev == myself
    outlier_order = jnp.cumsum(outlier_here.astype(jnp.int32)) - 1
    slot_match = outlier_here[None, :] & (
        outlier_order[None, :] == jnp.arange(OMOST, dtype=jnp.int32)[:, None]
    )
    outlier_local = jnp.sum(jnp.where(slot_match, outliers[None, :] - shard_base, 0), axis=1)
    outlier_live = jnp.any(slot_match, axis=1)
    key_blocks = cache_keys.reshape(spans_dev, SPAN, KVH, HD)
    out_keys = key_blocks[outlier_local[None, :], :, head_ids[:, None], :]
    out_pos = (outlier_local + shard_base)[:, None] * SPAN + jnp.arange(SPAN, dtype=jnp.int32)
    out_keys = rotate(out_keys.astype(jnp.float32), out_pos).astype(jnp.bfloat16)
    out_values = value_blocks[outlier_local[None, :], :, head_ids[:, None], :]
    slot_total = most_slots + OMOST
    slot_keys = jnp.concatenate(
        [sel_keys, jnp.broadcast_to(out_keys[None], (steps, KVH, OMOST, SPAN, HD))], axis=2
    )
    slot_values = jnp.concatenate(
        [sel_values, jnp.broadcast_to(out_values[None], (steps, KVH, OMOST, SPAN, HD))], axis=2
    )
    slot_live = jnp.concatenate(
        [is_live, jnp.broadcast_to(outlier_live[None, None], (steps, KVH, OMOST))], axis=2
    )
    step_pos = length + jnp.arange(steps, dtype=jnp.int32)
    query_rows = rotate(queries.reshape(steps, QH, HD).astype(jnp.float32), step_pos[:, None])
    own_queries = lax.dynamic_slice_in_dim(query_rows, myself * per_device, per_device, 1)
    grouped = query_rows.reshape(steps, KVH, group_size, HD)
    flat_keys = slot_keys.reshape(steps, KVH, slot_total * SPAN, HD)
    flat_values = slot_values.reshape(steps, KVH, slot_total * SPAN, HD)
    token_live = jnp.repeat(slot_live, SPAN, axis=2)
    local_stats = softmax_part(grouped, flat_keys, flat_values, token_live)
    merged = merged_2(local_stats, "seq", combine)
    run_max = lax.dynamic_slice_in_dim(
        merged[0].reshape(steps, QH), myself * per_device, per_device, 1
    )
    run_sum = lax.dynamic_slice_in_dim(
        merged[1].reshape(steps, QH), myself * per_device, per_device, 1
    )
    run_out = lax.dynamic_slice_in_dim(
        merged[2].reshape(steps, QH, HD), myself * per_device, per_device, 1
    )
    own_head = myself * per_device // group_size
    new_keys = lax.dynamic_index_in_dim(
        fresh_keys.reshape(steps, KVH, HD), own_head, 1, keepdims=False
    )
    new_keys = rotate(new_keys.astype(jnp.float32), step_pos).astype(jnp.bfloat16)
    new_values = lax.dynamic_index_in_dim(
        fresh_values.reshape(steps, KVH, HD), own_head, 1, keepdims=False
    )
    score_scale = 1.0 / jnp.sqrt(jnp.float32(HD))
    new_scores = (
        jnp.einsum(
            "thd,sd->ths",
            own_queries,
            new_keys.astype(jnp.float32),
            precision=lax.Precision.HIGHEST,
        )
        * score_scale
    )
    causal = jnp.arange(steps)[None, :] <= jnp.arange(steps)[:, None]
    new_scores = jnp.where(causal[:, None, :], new_scores, -1e30)
    joint_max = jnp.maximum(run_max, jnp.max(new_scores, axis=-1))
    old_scale = jnp.exp(run_max - joint_max)
    new_weights = jnp.exp(new_scores - joint_max[..., None]) * causal[:, None, :]
    summed = run_out * old_scale[..., None] + jnp.einsum(
        "ths,sd->thd", new_weights, new_values.astype(jnp.float32), precision=lax.Precision.HIGHEST
    )
    totals = run_sum * old_scale + jnp.sum(new_weights, axis=-1)
    attended = (summed / totals[..., None]).reshape(steps, per_device * HD).astype(jnp.bfloat16)
    return (attended, key_factor)


def solution(mesh):
    in_specs = (
        P(("groups", "seq"), None),
        P(("groups", "seq"), None),
        P(),
        P("groups", None),
        P("groups", None),
        P("groups", None),
        P("groups", None, None),
        P("groups", None, None),
        P("groups"),
    )
    out_specs = (P("groups", "seq"), P(("groups", "seq"), None))
    return jax.shard_map(
        on_device, mesh=mesh, in_specs=in_specs, out_specs=out_specs, check_vma=False
    )
```

profile of v0, /device:TPU:0, one launch (start us, length us, event | category | flops | bytes accessed | tf_op | source)
XLA Modules:
  0.0 299.0 jit_solution(4955914066819933756)
XLA Ops:
  7.2 15.1 %fusion.89 = f32[1024,1024]{1,0:T(8,128)} fusion(bf16[4096,1024]{1,0:T(8,128)(2,1)} %param.11), kind=kOutput, calls=%fused_computation.175 | convolution fusion | flops 8589934592 | bytes 12582912 | tf_op jit(solution)/shard_map/dot_general | solution.py:102
  23.4 9.1 %gather_fusion.4 = s32[1152]{0:T(1024)S(1)} fusion(s32[3,8,304]{2,1,0:T(8,128)S(1)} %concatenate.47, s32[1152]{0:T(1024)S(1)} %reshape.400), kind=kCustom, calls=%fused_computation.4 | custom fusion | bytes 23040 | tf_op jit(solution)/shard_map/jit(take_along_axis)/gather | solution.py:121
  33.5 4.5 %gather_fusion.1 = bf16[32,8,128]{2,1,0:T(8,128)(2,1)S(1)} fusion(bf16[512,8,8,128]{3,1,2,0:T(8,128)(2,1)} %bitcast.140, s32[32]{0:T(128)S(1)} %reshape.382), kind=kCustom, calls=%fused_computation.1 | custom fusion | bytes 131328 | tf_op jit(solution)/shard_map/gather | solution.py:143
  39.4 5.1 %gather_fusion.3 = bf16[32,8,128]{2,1,0:T(8,128)(2,1)} fusion(bf16[512,8,8,128]{3,1,2,0:T(8,128)(2,1)} %bitcast.145, s32[32]{0:T(128)S(1)} %reshape.382), kind=kCustom, calls=%fused_computation.3 | custom fusion | bytes 131328 | tf_op jit(solution)/shard_map/gather | solution.py:146
  44.5 15.0 %gather_fusion.2 = bf16[1152,8,128]{2,1,0:T(8,128)(2,1)} fusion(bf16[512,8,8,128]{3,1,2,0:T(8,128)(2,1)} %bitcast.146, s32[1152]{0:T(1024)S(1)} %reshape.388), kind=kCustom, calls=%fused_computation.2 | custom fusion | bytes 4727808 | tf_op jit(solution)/shard_map/gather | solution.py:134
  62.8 35.3 %reduce-scatter.2.cloned.1.call-done = f32[64,1024]{1,0:T(8,128)} async-done(((f32[1024,1024]{1,0:T(8,128)}), f32[64,1024]{1,0:T(8,128)}) %reduce-scatter.2.cloned.1.call-update) | async-done | bytes 262160 | tf_op jit(solution)/shard_map/reduce_scatter | solution.py:101
  98.1 1.7 fusion.36
  99.8 22.3 %all_gather.21 = f32[1024,160]{1,0:T(8,128)S(1)} all-gather(f32[64,160]{1,0:T(8,128)S(1)} %fusion.36), channel_id=1, replica_groups=mesh['groups'=2,'seq'=16] {'seq'}, dimensions={0}, use_global_device_ids=true | all-gather | bytes 696320 | tf_op jit(solution)/shard_map/all_gather | solution.py:110
  122.1 1.9 fusion.90
  124.1 11.7 %cholesky.51 = f32[128,128]{1,0:T(8,128)S(1)} custom-call(f32[128,128]{1,0:T(8,128)S(1)} %cholesky.124), custom_call_target="Cholesky" | custom-call | tf_op jit(solution)/shard_map/jit(cholesky)/cholesky | solution.py:40
  135.9 9.8 %custom-call.14 = f32[1,128,128]{1,2,0:T(8,128)S(1)} custom-call(f32[1,128,128]{2,1,0:T(8,128)S(1)} %get-tuple-element.236), custom_call_target="InvertDiagBlocksLowerTriangular" | custom-call | tf_op jit(solution)/shard_map/jit(cholesky)/cholesky | solution.py:40
  146.0 2.9 cholesky.110
  151.7 20.1 %custom-call.15 = f32[2,128,128]{1,2,0:T(8,128)S(1)} custom-call(f32[2,128,128]{2,1,0:T(8,128)S(1)} %pad_maximum_fusion.3), custom_call_target="InvertDiagBlocksLowerTriangular" | custom-call | tf_op jit(solution)/shard_map/triangular_solve | solution.py:41
  174.1 6.3 %convolution_bitcast_fusion = f32[4096,160]{0,1:T(8,128)S(1)} fusion(bf16[4096,1024]{1,0:T(8,128)(2,1)} %param.11, bf16[32,1024]{1,0:T(8,128)(2,1)S(1)} %convolution_convert_fusion, bf16[128,1024]{1,0:T(8,128)(2,1)S(1)} %get-tuple-element.249), kind=kOutput, calls=%fused_computation.21 | convolution fusion | flops 1342832640 | bytes 11337728 | tf_op jit(solution)/shard_map/dot_general | solution.py:113
  181.2 3.3 %copy.41 = f32[4096,160]{1,0:T(8,128)} copy(f32[4096,160]{0,1:T(8,128)S(1)} %convolution_bitcast_fusion) | data formatting | bytes 5242880 | tf_op jit(solution)/shard_map/dot_general | solution.py:113
  184.6 1.8 copy.55
  186.3 10.0 %gather_fusion = f32[1152,8,160]{2,1,0:T(8,128)} fusion(f32[512,8,160]{2,1,0:T(8,128)} %bitcast.136, s32[2048]{0:T(1024)} %pad_clamp_fusion), kind=kCustom, calls=%fused_computation | custom fusion | bytes 11801088 | tf_op jit(solution)/shard_map/gather | solution.py:125
  196.3 11.9 %fusion.19 = f32[3,8,48,8,128]{4,2,3,0,1:T(8,128)S(1)} fusion(f32[3,8,48,8,160]{4,3,2,1,0:T(8,128)} %bitcast.137, bf16[8,128,160,1,1]{1,0,2,4,3:T(8,128)(2,1)} %bitcast.143), kind=kOutput, calls=%fused_computation.34 | convolution fusion | flops 2264924160 | bytes 10944512 | tf_op jit(solution)/shard_map/tgmcr,gdr->tgmcd/dot_general | solution.py:127
  208.2 19.4 %fusion.10 = (bf16[3,8,48,8,64]{4,2,3,0,1:T(8,128)(2,1)S(1)}, bf16[3,8,48,8,64]{4,2,3,0,1:T(8,128)(2,1)S(1)}) fusion(f32[3,8,48,8,128]{4,2,3,0,1:T(8,128)S(1)} %fusion.19, f32[64]{0:T(128)S(1)} %multiply_exponential_fusion, f32[3,8,48,8]{2,3,0,1:T(8,128)S(1)} %copy-done.3), kind=kLoop, calls=%fused_computation.23 | loop fusion | flops 5308416 | bytes 7115008 | tf_op jit(solution)/shard_map/convert.11
  229.2 3.0 fusion.87
  232.2 2.2 fusion.13
  235.0 19.1 %all-gather.1 = f32[48,8,8]{2,1,0:T(8,128)S(1)} all-gather(f32[3,8,8]{2,1,0:T(8,128)S(1)} %fusion.35), channel_id=3, replica_groups=mesh['groups'=2,'seq'=16] {'seq'}, dimensions={0}, use_global_device_ids=true | all-gather | bytes 13056 | tf_op jit(solution)/shard_map/all_gather | solution.py:14
  254.1 18.6 %all-gather = f32[48,8,8]{2,1,0:T(8,128)S(1)} all-gather(f32[3,8,8]{2,1,0:T(8,128)S(1)} %get-tuple-element.251), channel_id=2, replica_groups=mesh['groups'=2,'seq'=16] {'seq'}, dimensions={0}, use_global_device_ids=true | all-gather | bytes 13056 | tf_op jit(solution)/shard_map/all_gather | solution.py:14
  273.7 16.3 %while.21 = (s32[]{:T(128)}, f32[3,8,8]{2,1,0:T(8,128)S(1)}, f32[3,8,8]{2,1,0:T(8,128)S(1)}, f32[3,8,8,128]{3,2,1,0:T(8,128)S(1)}, f32[16,3,8,8]{3,2,1,0:T(8,128...) while((s32[]{:T(128)}, f32[3,8,8]{2,1,0:T(8,128)S(1)}, ...), condition=%wide.region_12.13_spmd, body=%wide.region_11.12_spmd.sunk | while | flops 74885 | bytes 302743 | solution.py:20
  (139 shorter events, 32.5 us)
Async XLA Ops:
  7.2 90.9 %copy-start = (f32[1024,160]{0,1:T(8,128)S(1)}, f32[1024,160]{0,1:T(8,128)}, u32[]{:S(2)}) copy-start(f32[1024,160]{0,1:T(8,128)} %param.13) | copy-start | bytes 1966084
  7.2 15.3 %copy-start.7 = (s32[3,8,16]{2,1,0:T(8,128)S(1)}, s32[3,8,16]{2,1,0:T(8,128)}, u32[]{:S(2)}) copy-start(s32[3,8,16]{2,1,0:T(8,128)} %param.18) | copy-start | bytes 4612
  7.2 16.2 %copy-start.8 = (s32[3,8,256]{2,1,0:T(8,128)S(1)}, s32[3,8,256]{2,1,0:T(8,128)}, u32[]{:S(2)}) copy-start(s32[3,8,256]{2,1,0:T(8,128)} %param.17) | copy-start | bytes 73732
  7.2 90.9 %reduce-scatter.2.cloned.1.call-start = ((), (), s32[]{:S(2)}) async-start(), calls=%async_computation.1 | async-start | bytes 4456448 | tf_op jit(solution)/shard_map/reduce_scatter | solution.py:101
  22.4 250.4 %all-gather.5.cloned.1.call-start = ((), (), s32[]{:S(2)}) async-start(), calls=%async_computation.2 | async-start | bytes 1671168 | tf_op jit(solution)/shard_map/all_gather | solution.py:14
  23.4 9.6 %copy-start.11 = (s32[32]{0:T(128)S(1)}, s32[32]{0:T(128)}, u32[]{:S(2)}) copy-start(s32[32]{0:T(128)} %param.19) | copy-start | bytes 388
  23.4 15.1 %copy-start.6 = (bf16[3,8192]{1,0:T(4,128)(2,1)S(1)}, bf16[3,8192]{1,0:T(4,128)(2,1)}, u32[]{:S(2)}) copy-start(bf16[3,8192]{1,0:T(4,128)(2,1)} %param.14) | copy-start | bytes 147460
  180.4 15.9 %copy-start.1 = (f32[4096,160]{0,1:T(8,128)}, f32[4096,160]{0,1:T(8,128)S(1)}, u32[]{:S(2)}) copy-start(f32[4096,160]{0,1:T(8,128)S(1)} %convolution_bitcast_fusion) | copy-start | bytes 7864324
  196.3 11.9 %copy-start.3 = (f32[3,8,48,8]{2,3,0,1:T(8,128)S(1)}, f32[3,8,48,8]{2,3,0,1:T(8,128)}, u32[]{:S(2)}) copy-start(f32[3,8,48,8]{2,3,0,1:T(8,128)} %add_convert_fusion.1) | copy-start | bytes 110596
  227.7 4.5 %copy-start.4 = (bf16[32,8,128]{2,1,0:T(8,128)(2,1)S(1)}, bf16[32,8,128]{2,1,0:T(8,128)(2,1)}, u32[]{:S(2)}) copy-start(bf16[32,8,128]{2,1,0:T(8,128)(2,1)} %gather_fusion.3) | copy-start | bytes 196612
  227.7 4.5 %copy-start.2 = (bf16[1152,8,128]{2,1,0:T(8,128)(2,1)S(1)}, bf16[1152,8,128]{2,1,0:T(8,128)(2,1)}, u32[]{:S(2)}) copy-start(bf16[1152,8,128]{2,1,0:T(8,128)(2,1)} %gather_fusion.2) | copy-start | bytes 7077892
  227.7 4.5 %copy-start.5 = (f32[3,8,416]{2,1,0:T(8,128)S(1)}, f32[3,8,416]{2,1,0:T(8,128)}, u32[]{:S(2)}) copy-start(f32[3,8,416]{2,1,0:T(8,128)} %convert_element_type.103) | copy-start | bytes 119812
  229.2 5.3 %copy-start.9 = (bf16[3,64]{1,0:T(4,128)(2,1)S(1)}, bf16[3,64]{1,0:T(4,128)(2,1)}, u32[]{:S(2)}) copy-start(bf16[3,64]{1,0:T(4,128)(2,1)} %get-tuple-element.239) | copy-start | bytes 1156
  229.2 5.3 %copy-start.10 = (bf16[3,64]{1,0:T(4,128)(2,1)S(1)}, bf16[3,64]{1,0:T(4,128)(2,1)}, u32[]{:S(2)}) copy-start(bf16[3,64]{1,0:T(4,128)(2,1)} %get-tuple-element.240) | copy-start | bytes 1156
Sparse Core Ops, SparseCore 0:
  22.5 75.5 reduce-scatter.1
  234.6 37.5 all-gather.4
where the time goes:
time: 303 us; the launch traced here: 299 us
  other arithmetic  89.4 us (30%)
  blocking collectives  60 us (20%)
  local copies, waits for them, and re-layouts  51.8 us (17%)
  matrix products  45.9 us (15%)
  waiting for transfers between devices  35.3 us (12%)
  between operations  16 us (5%)
    all_gather x2, blocking collectives, merged_2(): everything = jax.tree.map(lambda part: lax.all_gather(part, axis), x)  37.8 us
    reduce_scatter x1, waiting for transfers between devices, on_device(): lax.psum_scatter(lax.dot_general(cache_keys, cache_keys, contract, prefer...  35.3 us
    another operation x7, other arithmetic, make_basis(): lower = jnp.linalg.cholesky(small_gram)  25.8 us
    all_gather x1, blocking collectives, on_device(): sketch = lax.all_gather(sketch_share, 'seq', axis=0, tiled=True)  22.3 us
    another operation x5, other arithmetic  20.3 us
    another operation x6, other arithmetic, make_basis(): lax.linalg.triangular_solve(lower, sketch.T, left_side=True, lower=True)  20.2 us
    add x15, other arithmetic, combine(): earlier[2] * scale_early[..., None] + later[2] * scale_late[..., None]  15.6 us
    dot_general x1, matrix products, on_device(): lax.dot_general(cache_keys, cache_keys, contract, preferred_element_type=...  15.1 us
  transfers between devices with their start and end apart: 2, of which 1 were waited for; matrix products, arithmetic and copies ran while one was open for 14% of the time, Pallas kernels for 0%

commit v1 on v0

v1 whole, which is shorter than its diff:
```python
import functools

import jax
import jax.numpy as jnp
from jax import lax
from jax.experimental import pallas as pl
from jax.experimental.pallas import tpu as pltpu
from jax.sharding import PartitionSpec as P

KVH = 8
HD = 128
QH = 64
SPAN = 8
OMOST = 4
HALF = HD // 2
LANES = 128
VMEM_LIMIT = 60 * 1024 * 1024
MESH = pl.DeviceIdType.MESH
NT = (((1,), (1,)), ((), ()))
NN = (((1,), (0,)), ((), ()))


def dot(a, b, dims=NN, precision=None):
    return lax.dot_general(a, b, dims, precision=precision, preferred_element_type=jnp.float32)


def pieces(x, count):
    parts = []
    for _ in range(count):
        part = x.astype(jnp.bfloat16)
        parts.append(part)
        x = x - part.astype(jnp.float32)
    return parts


def vmem(shape=None, index=None):
    if shape is None:
        return pl.BlockSpec(memory_space=pltpu.VMEM)
    return pl.BlockSpec(shape, index)


def sketch_kernel(length, s_ref, k_ref, out_ref, terms, acc):
    step = pl.program_id(0)
    rank = s_ref.shape[0]

    @pl.when(step == 0)
    def _():
        for i, part in enumerate(pieces(s_ref[...], 3)):
            terms[i * rank : (i + 1) * rank, :] = part

    keys = k_ref[...]
    wide = dot(terms[...], keys, NT)
    coords = wide[:rank] + wide[rank : 2 * rank] + wide[2 * rank :]
    high, low = pieces(coords, 2)
    share = dot(high, keys) + dot(low, keys)

    @pl.when(step == 0)
    def _():
        acc[...] = share

    @pl.when(step > 0)
    def _():
        acc[...] = acc[...] + share

    @pl.when(step == pl.num_programs(0) - 1)
    def _():
        total = acc[...] / length
        for c in range(out_ref.shape[1]):
            out_ref[:, c, :] = total[:, c * LANES : (c + 1) * LANES]


def sketch_part(s_t, cache_keys, length):
    rank, width = s_t.shape
    chunk = min(1024, cache_keys.shape[0])
    return pl.pallas_call(
        functools.partial(sketch_kernel, length),
        grid=(cache_keys.shape[0] // chunk,),
        out_shape=jax.ShapeDtypeStruct((rank, width // LANES, LANES), jnp.float32),
        in_specs=[vmem((rank, width), lambda i: (0, 0)), vmem((chunk, width), lambda i: (i, 0))],
        out_specs=vmem((rank, width // LANES, LANES), lambda i: (0, 0, 0)),
        scratch_shapes=[
            pltpu.VMEM((3 * rank, width), jnp.bfloat16),
            pltpu.VMEM((rank, width), jnp.float32),
        ],
        compiler_params=pltpu.CompilerParams(vmem_limit_bytes=VMEM_LIMIT),
        name="sketch_part",
    )(s_t, cache_keys)


def sum_kernel(
    chips, x_ref, out_ref, from_core, staged, inbox, full,
    core_s, core_r, chip_s, chip_r, back_s, back_r, fwd_s, fwd_r,
):
    me = lax.axis_index("seq")
    core = lax.rem(me, 2)
    chip = me // 2
    other = 1 - core
    partner = {"seq": chip * 2 + other}

    def chip_at(off):
        return lax.rem(chip + off, chips)

    def peer(off):
        return {"seq": chip_at(off) * 2 + core}

    barrier = pltpu.get_barrier_semaphore()
    pl.semaphore_signal(barrier, inc=1, device_id=partner, device_id_type=MESH)
    for off in range(1, chips):
        pl.semaphore_signal(barrier, inc=1, device_id=peer(off), device_id_type=MESH)
    pl.semaphore_wait(barrier, chips)

    def remote(src, dst, send, recv, target):
        return pltpu.make_async_remote_copy(
            src_ref=src, dst_ref=dst, send_sem=send, recv_sem=recv,
            device_id=target, device_id_type=MESH,
        )

    order = list(range(1, chips)) + [0]
    crossed = {}
    for off in order:
        crossed[off] = remote(
            x_ref.at[other, chip_at(off)], from_core.at[off], core_s.at[off], core_r.at[off], partner
        )
        crossed[off].start()
    sent = {}
    for off in order:
        crossed[off].wait_recv()
        staged[off] = x_ref[core, chip_at(off)] + from_core[off]
        if off:
            sent[off] = remote(
                staged.at[off], inbox.at[off], chip_s.at[off], chip_r.at[off], peer(off)
            )
            sent[off].start()
    total = staged[0]
    for off in range(1, chips):
        sent[off].wait_recv()
        total = total + inbox[off]
    full[core, chip] = total
    back = {}
    for off in range(1, chips):
        back[off] = remote(
            full.at[core, chip], full.at[core, chip], back_s.at[off], back_r.at[off], peer(off)
        )
        back[off].start()
    forward = {}
    for off in range(chips):
        source = chip_at(chips - off)
        if off:
            pltpu.make_async_remote_copy(
                src_ref=full.at[core, source], dst_ref=full.at[core, source],
                send_sem=back_s.at[off], recv_sem=back_r.at[off],
                device_id=peer(off), device_id_type=MESH,
            ).wait_recv()
        forward[off] = remote(
            full.at[core, source], full.at[core, source], fwd_s.at[off], fwd_r.at[off], partner
        )
        forward[off].start()
    for off in range(chips):
        source = chip_at(chips - off)
        pltpu.make_async_remote_copy(
            src_ref=full.at[other, source], dst_ref=full.at[other, source],
            send_sem=fwd_s.at[off], recv_sem=fwd_r.at[off],
            device_id=partner, device_id_type=MESH,
        ).wait_recv()
    out_ref[...] = full[...]
    for off in range(chips):
        crossed[off].wait_send()
        forward[off].wait_send()
        if off:
            sent[off].wait_send()
            back[off].wait_send()


def sum_over_seq(x, devices):
    chips = devices // 2
    shape = (2, chips, x.shape[0] // devices) + x.shape[1:]
    block = shape[1:]
    dma = pltpu.SemaphoreType.DMA((chips,))
    summed = pl.pallas_call(
        functools.partial(sum_kernel, chips),
        out_shape=jax.ShapeDtypeStruct(shape, jnp.float32),
        in_specs=[vmem()],
        out_specs=vmem(),
        scratch_shapes=[
            pltpu.VMEM(block, jnp.float32),
            pltpu.VMEM(block, jnp.float32),
            pltpu.VMEM(block, jnp.float32),
            pltpu.VMEM(shape, jnp.float32),
        ]
        + [dma] * 8,
        compiler_params=pltpu.CompilerParams(
            collective_id=0, has_side_effects=True, vmem_limit_bytes=VMEM_LIMIT
        ),
        name="sketch_sum",
    )(x.reshape(shape))
    return summed.reshape(x.shape)


def basis_kernel(sk_ref, basis_ref, split_ref, sk, a_ref, e_ref, inv_ref):
    rank = sk.shape[0]
    block = 32 if rank % 32 == 0 else 8
    high = lax.Precision.HIGHEST
    for c in range(sk_ref.shape[1]):
        sk[:, c * LANES : (c + 1) * LANES] = sk_ref[:, c, :]
    a_ref[...] = dot(sk[...], sk[...], NT, high)
    row = lax.broadcasted_iota(jnp.int32, (rank, rank), 0)
    column = lax.broadcasted_iota(jnp.int32, (rank, rank), 1)
    e_ref[...] = jnp.where(row == column, 1.0, 0.0)
    local = lax.broadcasted_iota(jnp.int32, (block, 1), 0)
    diagonal = lax.broadcasted_iota(jnp.int32, (block, rank), 1) - lax.broadcasted_iota(
        jnp.int32, (block, rank), 0
    )
    for top in range(0, rank, block):
        a = a_ref[top : top + block, :]
        e = e_ref[top : top + block, :]
        for j in range(block):
            pivot = a[j : j + 1, top + j : top + j + 1]
            factor = jnp.where(local > j, a[:, top + j : top + j + 1] / pivot, 0.0)
            a = a - factor * a[j : j + 1, :]
            e = e - factor * e[j : j + 1, :]
        pivots = jnp.sum(jnp.where(diagonal == top, a, 0.0), axis=1, keepdims=True)
        scale = 1.0 / jnp.sqrt(pivots)
        a = a * scale
        e = e * scale
        inv_ref[top : top + block, :] = e
        low = top + block
        if low < rank:
            a_t = a.T[low:, :]
            a_ref[low:, :] -= dot(a_t, a, NN, high)
            e_ref[low:, :] -= dot(a_t, e, NN, high)
    basis = dot(inv_ref[...], sk[...], NN, high)
    basis_ref[...] = basis.astype(jnp.bfloat16)
    for p in range(basis.shape[1] // (2 * HD)):
        pair = basis[:, p * 2 * HD : (p + 1) * 2 * HD]
        split_ref[:, p * 2 * HD : (p + 1) * 2 * HD] = jnp.concatenate(
            [
                pair[:, :HALF],
                pair[:, HD : HD + HALF],
                pair[:, HALF:HD],
                pair[:, HD + HALF :],
            ],
            axis=1,
        ).astype(jnp.bfloat16)


def make_basis(sketch_t):
    rank = sketch_t.shape[0]
    width = sketch_t.shape[1] * LANES
    shape = jax.ShapeDtypeStruct((rank, width), jnp.bfloat16)
    return pl.pallas_call(
        basis_kernel,
        out_shape=(shape, shape),
        in_specs=[vmem()],
        out_specs=(vmem(), vmem()),
        scratch_shapes=[
            pltpu.VMEM((rank, width), jnp.float32),
            pltpu.VMEM((rank, rank), jnp.float32),
            pltpu.VMEM((rank, rank), jnp.float32),
            pltpu.VMEM((rank, rank), jnp.float32),
        ],
        compiler_params=pltpu.CompilerParams(vmem_limit_bytes=VMEM_LIMIT),
        name="key_basis",
    )(sketch_t)


def attend_kernel(
    k_ref, v_ref, basis_ref, split_ref, q_ref, live_ref, ca_ref, sa_ref, cb_ref, sb_ref,
    xk_ref, xv_ref, xlive_ref, factor_ref, out_ref, max_ref, sum_ref, terms, spread,
):
    step = pl.program_id(0)
    pairs, rows, width = q_ref.shape
    chunk = k_ref.shape[0]
    spans = spread.shape[0]

    @pl.when(step == 0)
    def _():
        for p in range(pairs):
            for i, part in enumerate(pieces(q_ref[p], 3)):
                terms[p, i * rows : (i + 1) * rows, :] = part
        token = lax.broadcasted_iota(jnp.int32, (spans, chunk), 1)
        span = lax.broadcasted_iota(jnp.int32, (spans, chunk), 0)
        spread[...] = jnp.where(token // SPAN == span, 1.0, 0.0).astype(jnp.bfloat16)
        out_ref[...] = jnp.zeros_like(out_ref)
        sum_ref[...] = jnp.zeros_like(sum_ref)
        max_ref[...] = jnp.full(max_ref.shape, -1e30, jnp.float32)

    def absorb(p, keys, values, live):
        here = slice(p * rows, (p + 1) * rows)
        wide = dot(terms[p], keys, NT)
        scores = wide[:rows] + wide[rows : 2 * rows] + wide[2 * rows :]
        scores = jnp.where(live > 0.5, scores, -1e30)
        before = max_ref[here, :]
        after = jnp.maximum(before, jnp.max(scores, axis=1, keepdims=True))
        weights = jnp.where(live > 0.5, jnp.exp(scores - after[:, :1]), 0.0)
        scale = jnp.exp(before - after)
        max_ref[here, :] = after
        sum_ref[here, :] = sum_ref[here, :] * scale + jnp.sum(weights, axis=1, keepdims=True)
        both = dot(jnp.concatenate(pieces(weights, 2), axis=0), values)
        both = both[:rows] + both[rows:]
        own = jnp.concatenate([both[: rows // 2, :HD], both[rows // 2 :, HD:]], axis=0)
        out_ref[here, :] = out_ref[here, :] * scale + own

    factor = dot(k_ref[...], basis_ref[...], NT)
    factor_ref[...] = factor
    high, low = pieces(factor, 2)
    cb, sb = cb_ref[...], sb_ref[...]
    cosine, sine = [], []
    for i in range(ca_ref.shape[0]):
        ca, sa = ca_ref[i : i + 1, :], sa_ref[i : i + 1, :]
        cosine.append(ca * cb - sa * sb)
        sine.append(sa * cb + ca * sb)
    cosine = jnp.concatenate(cosine, axis=0)
    sine = jnp.concatenate(sine, axis=0)
    for p in range(pairs):
        columns = slice(p * width, (p + 1) * width)
        rebuilt = dot(high, split_ref[:, columns]) + dot(low, split_ref[:, columns])
        first, second = rebuilt[:, :HD], rebuilt[:, HD:]
        keys = jnp.concatenate(
            [first * cosine - second * sine, second * cosine + first * sine], axis=1
        ).astype(jnp.bfloat16)
        live = dot(live_ref[p * rows : (p + 1) * rows, :], spread[...])
        absorb(p, keys, v_ref[:, columns], live)

    @pl.when(step == pl.num_programs(0) - 1)
    def _():
        for p in range(pairs):
            columns = slice(p * width, (p + 1) * width)
            live = xlive_ref[p * rows : (p + 1) * rows, :]
            absorb(p, xk_ref[:, columns], xv_ref[:, columns], live)


def attend(cache_keys, cache_values, basis, split, q, live, tables, xk, xv, xlive):
    seq_len, width = cache_keys.shape
    rank = basis.shape[0]
    pairs, rows, pair_width = q.shape
    chunk = min(LANES * SPAN, seq_len)
    spans = chunk // SPAN
    fine = tables[2].shape[0]
    total = pairs * rows
    whole = lambda *shape: vmem(shape, lambda i: (0,) * len(shape))
    stat = jax.ShapeDtypeStruct((total, LANES), jnp.float32)
    return pl.pallas_call(
        attend_kernel,
        grid=(seq_len // chunk,),
        out_shape=(jax.ShapeDtypeStruct((seq_len, rank), jnp.float32), stat, stat, stat),
        in_specs=[
            vmem((chunk, width), lambda i: (i, 0)),
            vmem((chunk, width), lambda i: (i, 0)),
            whole(rank, width),
            whole(rank, width),
            whole(pairs, rows, pair_width),
            vmem((total, spans), lambda i: (0, i)),
            vmem((chunk // fine, LANES), lambda i: (i, 0)),
            vmem((chunk // fine, LANES), lambda i: (i, 0)),
            whole(fine, LANES),
            whole(fine, LANES),
            whole(*xk.shape),
            whole(*xv.shape),
            whole(*xlive.shape),
        ],
        out_specs=(vmem((chunk, rank), lambda i: (i, 0)),) + (whole(total, LANES),) * 3,
        scratch_shapes=[
            pltpu.VMEM((pairs, 3 * rows, pair_width), jnp.bfloat16),
            pltpu.VMEM((spans, chunk), jnp.bfloat16),
        ],
        compiler_params=pltpu.CompilerParams(vmem_limit_bytes=VMEM_LIMIT),
        name="attend",
    )(cache_keys, cache_values, basis, split, q, live, *tables, xk, xv, xlive)


def merge_kernel(devices, x_ref, out_ref, inbox, send_sem, recv_sem):
    me = lax.axis_index("seq")
    rows = out_ref.shape[0]

    def peer(off):
        return lax.rem(me + off, devices)

    barrier = pltpu.get_barrier_semaphore()
    for off in range(1, devices):
        pl.semaphore_signal(
            barrier, inc=1, device_id={"seq": peer(off)}, device_id_type=MESH
        )
    pl.semaphore_wait(barrier, devices - 1)
    copies = []
    for off in range(1, devices):
        copy = pltpu.make_async_remote_copy(
            src_ref=x_ref.at[peer(off)], dst_ref=inbox.at[off],
            send_sem=send_sem.at[off], recv_sem=recv_sem.at[off],
            device_id={"seq": peer(off)}, device_id_type=MESH,
        )
        copy.start()
        copies.append(copy)
    own = x_ref[me]
    for copy in copies:
        copy.wait_recv()
    blocks = [own] + [inbox[off] for off in range(1, devices)]
    maxima = [block[rows:, :1] for block in blocks]
    joint = functools.reduce(jnp.maximum, maxima)
    total = jnp.zeros((rows, 1), jnp.float32)
    summed = jnp.zeros((rows, HD), jnp.float32)
    for block, top in zip(blocks, maxima):
        scale = jnp.exp(top - joint)
        total = total + block[rows:, HALF : HALF + 1] * scale
        summed = summed + block[:rows, :] * scale
    out_ref[...] = (summed / total).astype(out_ref.dtype)
    for copy in copies:
        copy.wait_send()


def merge(x):
    devices, rows, lanes = x.shape
    return pl.pallas_call(
        functools.partial(merge_kernel, devices),
        out_shape=jax.ShapeDtypeStruct((rows // 2, lanes), jnp.bfloat16),
        in_specs=[vmem()],
        out_specs=vmem(),
        scratch_shapes=[
            pltpu.VMEM(x.shape, jnp.float32),
            pltpu.SemaphoreType.DMA((devices,)),
            pltpu.SemaphoreType.DMA((devices,)),
        ],
        compiler_params=pltpu.CompilerParams(collective_id=1, has_side_effects=True),
        name="merge",
    )(x)


def waves(positions):
    exponents = jnp.arange(HALF, dtype=jnp.float32) * (2.0 / HD)
    inverse_freq = jnp.exp(-jnp.log(jnp.float32(500000.0)) * exponents)
    angles = positions.astype(jnp.float32)[..., None] * inverse_freq
    return jnp.cos(angles), jnp.sin(angles)


def rotate_halves(vectors, positions):
    cosine, sine = waves(positions)
    first, second = vectors[..., :HALF], vectors[..., HALF:]
    return jnp.stack([first * cosine - second * sine, second * cosine + first * sine], axis=-2)


def on_device(
    cache_keys,
    cache_values,
    sketch_matrix,
    queries,
    fresh_keys,
    fresh_values,
    chosen,
    shard_counts,
    outliers,
):
    seq_len, width = cache_keys.shape
    devices = lax.axis_size("seq")
    myself = lax.axis_index("seq")
    length = seq_len * devices
    steps = queries.shape[0]
    group = QH // KVH
    per_device = QH // devices
    pairs = KVH // 2
    spans_dev = seq_len // SPAN
    base = myself * spans_dev

    share = sketch_part(sketch_matrix.T, cache_keys, length)
    basis, split = make_basis(sum_over_seq(share, devices))

    own_spans = base + jnp.arange(spans_dev, dtype=jnp.int32)
    live = jnp.any(chosen[..., None] == own_spans, axis=2)
    live = jnp.broadcast_to(
        live.transpose(1, 0, 2)[:, :, None, :], (KVH, steps, group, spans_dev)
    ).reshape(KVH * steps * group, spans_dev).astype(jnp.bfloat16)

    outlier_here = outliers // spans_dev == myself
    order = jnp.cumsum(outlier_here.astype(jnp.int32)) - 1
    match = outlier_here & (order == jnp.arange(OMOST, dtype=jnp.int32)[:, None])
    local = jnp.sum(jnp.where(match, outliers - base, 0), axis=1)
    outlier_live = jnp.any(match, axis=1)
    exact = [lax.dynamic_slice_in_dim(cache_keys, local[i] * SPAN, SPAN, 0) for i in range(OMOST)]
    exact_v = [
        lax.dynamic_slice_in_dim(cache_values, local[i] * SPAN, SPAN, 0) for i in range(OMOST)
    ]
    step_pos = length + jnp.arange(steps, dtype=jnp.int32)
    token = jnp.arange(SPAN, dtype=jnp.int32)
    extra_pos = jnp.concatenate([((local + base)[:, None] * SPAN + token).reshape(-1), step_pos])
    count = OMOST * SPAN + steps
    pad = ((0, LANES - count), (0, 0))
    xk = jnp.concatenate(exact + [fresh_keys], axis=0).reshape(count, KVH, HD)
    xk = rotate_halves(xk.astype(jnp.float32), extra_pos[:, None])
    xk = xk.reshape(count, pairs, 2, 2, HALF).transpose(0, 1, 3, 2, 4).reshape(count, width)
    xk = jnp.pad(xk.astype(jnp.bfloat16), pad)
    xv = jnp.pad(jnp.concatenate(exact_v + [fresh_values], axis=0), pad)
    causal = jnp.arange(steps)[None, :] <= jnp.arange(steps)[:, None]
    extra_live = jnp.concatenate(
        [
            jnp.broadcast_to(jnp.repeat(outlier_live, SPAN), (steps, OMOST * SPAN)),
            causal & (myself == 0),
        ],
        axis=1,
    )
    xlive = jnp.pad(extra_live.astype(jnp.float32), ((0, 0), (0, LANES - count)))
    xlive = jnp.broadcast_to(
        xlive[None, :, None, :], (KVH, steps, group, LANES)
    ).reshape(KVH * steps * group, LANES)

    score_scale = 1.0 / jnp.sqrt(jnp.float32(HD))
    q = rotate_halves(queries.reshape(steps, QH, HD).astype(jnp.float32), step_pos[:, None])
    q = (q * score_scale).reshape(steps, pairs, 2, group, 2, HALF).transpose(1, 2, 0, 3, 4, 5)
    own_lane = jnp.eye(2, dtype=jnp.float32)[None, :, None, None, None, :, None]
    q = (q[:, :, :, :, :, None, :] * own_lane).reshape(pairs, 2 * steps * group, 2 * HD)

    fine = 64
    coarse = jnp.arange(seq_len // fine, dtype=jnp.int32) * fine + myself * seq_len
    tables = waves(coarse) + waves(jnp.arange(fine, dtype=jnp.int32))
    tables = [jnp.concatenate([table, table], axis=1) for table in tables]

    key_factor, out, top, total = attend(
        cache_keys, cache_values, basis, split, q, live, tables, xk, xv, xlive
    )

    def deal(x):
        x = x.reshape(KVH, steps, group // per_device, per_device, LANES)
        return x.transpose(0, 2, 1, 3, 4).reshape(devices, steps * per_device, LANES)

    stats = jnp.where(jnp.arange(LANES) < HALF, top, total)
    attended = merge(jnp.concatenate([deal(out), deal(stats)], axis=1))
    return (attended.reshape(steps, per_device * HD), key_factor)


def solution(mesh):
    in_specs = (
        P(("groups", "seq"), None),
        P(("groups", "seq"), None),
        P(),
        P("groups", None),
        P("groups", None),
        P("groups", None),
        P("groups", None, None),
        P("groups", None, None),
        P("groups"),
    )
    out_specs = (P("groups", "seq"), P(("groups", "seq"), None))
    return jax.shard_map(
        on_device, mesh=mesh, in_specs=in_specs, out_specs=out_specs, check_vma=False
    )
```

time: 303 us -> 128 us (0.42); the launches traced: 299 us -> 127 us
  Pallas kernels: 0 us -> 93.8 us
  other arithmetic: 89.4 us -> 11 us
  blocking collectives: 60 us -> 0 us
  matrix products: 45.9 us -> 0 us
  waiting for transfers between devices: 35.3 us -> 0 us
  local copies, waits for them, and re-layouts: 51.8 us -> 18.9 us
  between operations: 16 us -> 3.43 us
    pallas_call x0 -> x5, Pallas kernels: none -> 93.8 us  [the longest x1 27.6 us: attend(): pl.pallas_call(attend_kernel, grid=(seq_len // chunk,), out_shape=(jax.Sh...]
    another operation x19 -> x3, other arithmetic: 66.9 us -> 0.84 us  [the longest x7 25.8 us: make_basis(): lower = jnp.linalg.cholesky(small_gram)]
    all_gather x3 -> x0, blocking collectives: 60 us -> none  [the longest x2 37.8 us: merged_2(): everything = jax.tree.map(lambda part: lax.all_gather(part, axis), x)]
    gather x8 -> x0, local copies, waits for them, and re-layouts: 43.8 us -> none  [the longest x1 15 us: on_device(): sel_values = value_blocks[local_span, :, head_ids[None, :, None], :]]
    dot_general x9 -> x0, matrix products: 43.3 us -> none  [the longest x1 15.1 us: on_device(): lax.dot_general(cache_keys, cache_keys, contract, preferred_element_type=...]
    reduce_scatter x1 -> x0, waiting for transfers between devices: 35.3 us -> none  [on_device(): lax.psum_scatter(lax.dot_general(cache_keys, cache_keys, contract, prefer...]
    add x31 -> x3, other arithmetic: 16 us -> 0.08 us  [the longest x1 0.07 us: on_device(): (local + base)[:, None] * SPAN + token]
    unnamed x27 -> x10, local copies, waits for them, and re-layouts: 2.44 us -> 10.1 us
  transfers between devices with their start and end apart: 2 -> 0, of which waited for: 1 -> 0; matrix products, arithmetic and copies ran while one was open for 14% -> 0% of each run, Pallas kernels for 0% -> 0%
where the time goes in v1:
time: 128 us; the launch traced here: 127 us
  Pallas kernels  93.8 us (73%)
  local copies, waits for them, and re-layouts  18.9 us (15%)
  other arithmetic  11 us (9%)
  between operations  3.43 us (3%)
    pallas_call x1, Pallas kernels, attend(): pl.pallas_call(attend_kernel, grid=(seq_len // chunk,), out_shape=(jax.Sh...  27.6 us
    pallas_call x1, Pallas kernels, sum_over_seq(): pl.pallas_call(functools.partial(sum_kernel, chips), out_shape=jax.ShapeD...  24.8 us
    pallas_call x1, Pallas kernels, make_basis(): pl.pallas_call(basis_kernel, out_shape=(shape, shape), in_specs=[vmem()],...  18.1 us
    pallas_call x1, Pallas kernels, merge(): pl.pallas_call(functools.partial(merge_kernel, devices), out_shape=jax.Sh...  12.3 us
    pallas_call x1, Pallas kernels, sketch_part(): pl.pallas_call(functools.partial(sketch_kernel, length), grid=(cache_keys...  11 us
    unnamed x10, local copies, waits for them, and re-layouts  10.1 us
    reduce_or x1, other arithmetic, on_device(): live = jnp.any(chosen[..., None] == own_spans, axis=2)  3.08 us

profile of v1, /device:TPU:0, one launch (start us, length us, event | category | flops | bytes accessed | tf_op | source)
XLA Modules:
  0.0 127.1 jit_solution(3690987896628218834)
XLA Ops:
  2.2 3.1 %compare_reduce_fusion = pred[3,8,512]{2,1,0:T(8,128)(4,1)S(1)} fusion(s32[512]{0:T(512)S(1)} %iota_add_fusion.1, s32[3,8,256]{2,1,0:T(8,128)} %param.15), kind=kLoop, calls=%fused_computation | loop fusion | flops 6279168 | bytes 38912 | tf_op jit(solution)/shard_map/reduce_or | solution.py:466
  10.9 0.7 pad_maximum_fusion.3
  12.3 0.9 convert_bitcast_fusion
  13.8 0.7 constant_dynamic-update-slice_fusion.4
  14.5 0.7 constant_dynamic-update-slice_fusion.3
  15.2 0.7 constant_dynamic-update-slice_fusion.8
  15.9 0.7 constant_dynamic-update-slice_fusion.7
  16.7 0.7 constant_dynamic-update-slice_fusion.2
  17.4 0.7 constant_dynamic-update-slice_fusion.1
  18.1 0.7 constant_dynamic-update-slice_fusion.6
  18.8 0.7 constant_dynamic-update-slice_fusion.5
  19.5 0.7 constant_dynamic-update-slice_fusion
  21.5 0.7 pad.14.xk_ref
  22.3 0.7 pad.15.xv_ref
  23.5 0.7 broadcast_multiply_fusion.q_ref
  24.3 11.0 %sketch_part.1 = f32[160,8,128]{2,1,0:T(8,128)} custom-call(f32[160,1024]{1,0:T(8,128)} %bitcast.41, bf16[4096,1024]{1,0:T(8,128)(2,1)} %k_ref.3), custom_call_target="tpu_custom_call" | custom-call | tf_op jit(solution)/shard_map/sketch_part/pallas_call | solution.py:75
  35.2 24.8 %sketch_sum.1 = f32[2,8,10,8,128]{4,3,2,1,0:T(8,128)} custom-call(f32[2,8,10,8,128]{4,3,2,1,0:T(8,128)} %bitcast.37), custom_call_target="tpu_custom_call" | custom-call | tf_op jit(solution)/shard_map/sketch_sum/pallas_call | solution.py:179
  60.0 18.1 %key_basis.1 = (bf16[160,1024]{1,0:T(8,128)(2,1)}, bf16[160,1024]{1,0:T(8,128)(2,1)}) custom-call(f32[160,8,128]{2,1,0:T(8,128)} %bitcast.38), custom_call_target="tpu_custom_call" | custom-call | tf_op jit(solution)/shard_map/key_basis/pallas_call | solution.py:250
  78.1 27.6 %attend.1 = (f32[4096,160]{1,0:T(8,128)}, f32[192,128]{1,0:T(8,128)}, f32[192,128]{1,0:T(8,128)}, f32[192,128]{1,0:T(8,128)}) custom-call(bf16[4096,1024]{1,0:T(8,128)(2,1)} %k_ref.3, bf16[4096,1024]{1,0:T(8,128)(2,1)} %v_ref.1, bf16[160,1024]{1,0:T(8,128)(2,1)} %get-tuple-element.8.basis_ref, bf16[160,1024]{1,0:T(8,128)(2,1)} %get-tuple-element.9.split_ref, ...), custom_call_target="tpu_custom_call" | custom-call | tf_op jit(solution)/shard_map/attend/pallas_call | solution.py:342
  105.7 0.9 copy.28
  106.7 1.0 broadcast_select_fusion
  108.4 12.3 %merge.1 = bf16[12,128]{1,0:T(8,128)(2,1)} custom-call(f32[16,24,128]{2,1,0:T(8,128)} %pad_maximum_fusion.x_ref), custom_call_target="tpu_custom_call" | custom-call | tf_op jit(solution)/shard_map/merge/pallas_call | solution.py:412
  120.8 1.3 %reshape.291 = bf16[3,512]{1,0:T(4,128)(2,1)} reshape(bf16[12,128]{1,0:T(8,128)(2,1)} %merge.1) | data formatting | bytes 6144 | tf_op jit(solution)/shard_map/reshape | solution.py:524
  122.1 5.1 %copy.32 = f32[4096,160]{0,1:T(8,128)} copy(f32[4096,160]{1,0:T(8,128)} %get-tuple-element.19) | data formatting | bytes 5242880
  (53 shorter events, 8.4 us)

commit v2 on v1

--- a/solution.py
+++ b/solution.py
@@ -13,6 +13,7 @@
 SPAN = 8
 OMOST = 4
 HALF = HD // 2
+FINE = 64
 LANES = 128
 VMEM_LIMIT = 60 * 1024 * 1024
 MESH = pl.DeviceIdType.MESH
@@ -263,35 +264,104 @@
     )(sketch_t)
 
 
+def split_pair(x):
+    first = jnp.concatenate([x[:, :HALF], x[:, HD : HD + HALF]], axis=1)
+    second = jnp.concatenate([x[:, HALF:HD], x[:, HD + HALF :]], axis=1)
+    return first, second
+
+
+def turn(first, second, cosine, sine):
+    return jnp.concatenate(
+        [first * cosine - second * sine, second * cosine + first * sine], axis=1
+    )
+
+
 def attend_kernel(
-    k_ref, v_ref, basis_ref, split_ref, q_ref, live_ref, ca_ref, sa_ref, cb_ref, sb_ref,
-    xk_ref, xv_ref, xlive_ref, factor_ref, out_ref, max_ref, sum_ref, terms, spread,
+    outl_ref, k_ref, v_ref, k_all, v_all, basis_ref, split_ref, q_ref, live_ref, cos_ref,
+    sin_ref, fresh_k, fresh_v, factor_ref, deal_ref,
+    terms, spread, widen, out_ref, max_ref, sum_ref, cosines, sines, xk_land, xv_land, xk, xv,
+    local_ref, sems,
 ):
     step = pl.program_id(0)
-    pairs, rows, width = q_ref.shape
+    steps = fresh_k.shape[0]
+    width = 2 * HD
+    pairs = k_ref.shape[1] // width
+    group = QH // KVH
+    list_rows = steps * group
+    rows = 2 * list_rows
     chunk = k_ref.shape[0]
     spans = spread.shape[0]
+    spans_dev = k_all.shape[0] // SPAN
+    coarse = spans_dev * SPAN // FINE
+    myself = lax.axis_index("seq")
+    base = myself * spans_dev
+    per_device = deal_ref.shape[1] // (2 * steps)
 
     @pl.when(step == 0)
     def _():
+        for i in range(OMOST + 1):
+            local_ref[i] = 0
+        found = jnp.int32(0)
+        for i in range(outl_ref.shape[0]):
+            span = outl_ref[i] - base
+            local_ref[found] = span
+            here = (span >= 0) & (span < spans_dev)
+            found = found + here.astype(jnp.int32)
+        copies = []
+        for j in range(OMOST):
+            at = jnp.where(j < found, local_ref[j], 0)
+            local_ref[j] = at
+            for n, (whole, land) in enumerate(((k_all, xk_land), (v_all, xv_land))):
+                copy = pltpu.make_async_copy(
+                    whole.at[pl.ds(pl.multiple_of(at * SPAN, SPAN), SPAN), :],
+                    land.at[j],
+                    sems.at[n, j],
+                )
+                copy.start()
+                copies.append(copy)
+        local_ref[OMOST] = found
+
+        cosines[...] = jnp.concatenate([cos_ref[...]] * 2, axis=1)
+        sines[...] = jnp.concatenate([sin_ref[...]] * 2, axis=1)
+        first_step = coarse + FINE
+        zeros = jnp.zeros((list_rows, HALF), jnp.float32)
         for p in range(pairs):
-            for i, part in enumerate(pieces(q_ref[p], 3)):
-                terms[p, i * rows : (i + 1) * rows, :] = part
+            for side in range(2):
+                head = (2 * p + side) * group
+                turned = []
+                for t in range(steps):
+                    x = q_ref[t * QH + head : t * QH + head + group, :]
+                    c = cos_ref[first_step + t : first_step + t + 1, :]
+                    d = sin_ref[first_step + t : first_step + t + 1, :]
+                    turned.append(turn(x[:, :HALF], x[:, HALF:], c, d))
+                x = jnp.concatenate(turned, axis=0)
+                x = [x[:, :HALF], zeros, x[:, HALF:], zeros]
+                if side:
+                    x = [x[1], x[0], x[3], x[2]]
+                for i, part in enumerate(pieces(jnp.concatenate(x, axis=1), 3)):
+                    at = i * rows + side * list_rows
+                    terms[p, at : at + list_rows, :] = part.astype(jnp.float32)
         token = lax.broadcasted_iota(jnp.int32, (spans, chunk), 1)
         span = lax.broadcasted_iota(jnp.int32, (spans, chunk), 0)
         spread[...] = jnp.where(token // SPAN == span, 1.0, 0.0).astype(jnp.bfloat16)
+        row = lax.broadcasted_iota(jnp.int32, widen.shape, 0)
+        which = lax.broadcasted_iota(jnp.int32, widen.shape, 1)
+        source = ((row % list_rows) // group) * KVH + row // list_rows
+        widen[...] = jnp.where(which == source, 1.0, 0.0).astype(jnp.bfloat16)
         out_ref[...] = jnp.zeros_like(out_ref)
         sum_ref[...] = jnp.zeros_like(sum_ref)
         max_ref[...] = jnp.full(max_ref.shape, -1e30, jnp.float32)
+        for copy in copies:
+            copy.wait()
 
     def absorb(p, keys, values, live):
         here = slice(p * rows, (p + 1) * rows)
-        wide = dot(terms[p], keys, NT)
+        wide = dot(terms[p].astype(jnp.bfloat16), keys, NT)
         scores = wide[:rows] + wide[rows : 2 * rows] + wide[2 * rows :]
-        scores = jnp.where(live > 0.5, scores, -1e30)
+        scores = jnp.where(live, scores, -1e30)
         before = max_ref[here, :]
         after = jnp.maximum(before, jnp.max(scores, axis=1, keepdims=True))
-        weights = jnp.where(live > 0.5, jnp.exp(scores - after[:, :1]), 0.0)
+        weights = jnp.where(live, jnp.exp(scores - after[:, :1]), 0.0)
         scale = jnp.exp(before - after)
         max_ref[here, :] = after
         sum_ref[here, :] = sum_ref[here, :] * scale + jnp.sum(weights, axis=1, keepdims=True)
@@ -301,71 +371,133 @@
         out_ref[here, :] = out_ref[here, :] * scale + own
 
     factor = dot(k_ref[...], basis_ref[...], NT)
-    factor_ref[...] = factor
+    factor_ref[...] = factor.T
     high, low = pieces(factor, 2)
-    cb, sb = cb_ref[...], sb_ref[...]
+    cb = cosines[coarse : coarse + FINE, :]
+    sb = sines[coarse : coarse + FINE, :]
     cosine, sine = [], []
-    for i in range(ca_ref.shape[0]):
-        ca, sa = ca_ref[i : i + 1, :], sa_ref[i : i + 1, :]
+    for i in range(chunk // FINE):
+        ca = cosines[pl.ds(step * (chunk // FINE) + i, 1), :]
+        sa = sines[pl.ds(step * (chunk // FINE) + i, 1), :]
         cosine.append(ca * cb - sa * sb)
         sine.append(sa * cb + ca * sb)
     cosine = jnp.concatenate(cosine, axis=0)
     sine = jnp.concatenate(sine, axis=0)
+    live_all = dot(widen[...], live_ref[...]).astype(jnp.bfloat16)
     for p in range(pairs):
         columns = slice(p * width, (p + 1) * width)
         rebuilt = dot(high, split_ref[:, columns]) + dot(low, split_ref[:, columns])
-        first, second = rebuilt[:, :HD], rebuilt[:, HD:]
-        keys = jnp.concatenate(
-            [first * cosine - second * sine, second * cosine + first * sine], axis=1
-        ).astype(jnp.bfloat16)
-        live = dot(live_ref[p * rows : (p + 1) * rows, :], spread[...])
-        absorb(p, keys, v_ref[:, columns], live)
+        keys = turn(rebuilt[:, :HD], rebuilt[:, HD:], cosine, sine).astype(jnp.bfloat16)
+        live = dot(live_all[p * rows : (p + 1) * rows, :], spread[...])
+        absorb(p, keys, v_ref[:, columns], live > 0.5)
 
     @pl.when(step == pl.num_programs(0) - 1)
     def _():
+        exact = OMOST * SPAN
+        xk[...] = jnp.zeros_like(xk)
+        xv[...] = jnp.zeros_like(xv)
+        for j in range(OMOST):
+            xk[j * SPAN : (j + 1) * SPAN, :] = xk_land[j].astype(jnp.float32)
+            xv[j * SPAN : (j + 1) * SPAN, :] = xv_land[j].astype(jnp.float32)
+        xk[exact : exact + steps, :] = fresh_k[...].astype(jnp.float32)
+        xv[exact : exact + steps, :] = fresh_v[...].astype(jnp.float32)
+        xc, xs = [], []
+        for j in range(OMOST):
+            at = local_ref[j] * SPAN
+            ca = cosines[pl.ds(at // FINE, 1), :]
+            sa = sines[pl.ds(at // FINE, 1), :]
+            near = pl.multiple_of(coarse + at % FINE, SPAN)
+            cb = cosines[pl.ds(near, SPAN), :]
+            sb = sines[pl.ds(near, SPAN), :]
+            xc.append(ca * cb - sa * sb)
+            xs.append(sa * cb + ca * sb)
+        rest = jnp.zeros((LANES - exact - SPAN, LANES), jnp.float32)
+        xc = jnp.concatenate(xc + [cosines[coarse + FINE :, :], rest], axis=0)
+        xs = jnp.concatenate(xs + [sines[coarse + FINE :, :], rest], axis=0)
+        row = lax.broadcasted_iota(jnp.int32, (rows, LANES), 0)
+        lane = lax.broadcasted_iota(jnp.int32, (rows, LANES), 1)
+        reach = jnp.where(myself == 0, exact, -LANES)
+        own_step = (row % list_rows) // group
+        live = (lane < local_ref[OMOST] * SPAN) | (
+            (lane >= exact) & (lane <= reach + own_step)
+        )
         for p in range(pairs):
             columns = slice(p * width, (p + 1) * width)
-            live = xlive_ref[p * rows : (p + 1) * rows, :]
-            absorb(p, xk_ref[:, columns], xv_ref[:, columns], live)
-
-
-def attend(cache_keys, cache_values, basis, split, q, live, tables, xk, xv, xlive):
+            first, second = split_pair(xk[:, columns])
+            keys = turn(first, second, xc, xs).astype(jnp.bfloat16)
+            absorb(p, keys, xv[:, columns].astype(jnp.bfloat16), live)
+        half = steps * per_device
+        lane = lax.broadcasted_iota(jnp.int32, out_ref.shape, 1)
+        max_ref[...] = jnp.where(lane < HALF, max_ref[...], sum_ref[...])
+        for device in range(deal_ref.shape[0]):
+            for t in range(steps):
+                head = device * per_device
+                at = (head // group) * list_rows + t * group + head % group
+                to = t * per_device
+                deal_ref[device, to : to + per_device, :] = out_ref[at : at + per_device, :]
+                deal_ref[device, half + to : half + to + per_device, :] = max_ref[
+                    at : at + per_device, :
+                ]
+
+
+def attend(cache_keys, cache_values, basis, split, q, live, cosine, sine, fresh_k, fresh_v, outliers, devices):
     seq_len, width = cache_keys.shape
     rank = basis.shape[0]
-    pairs, rows, pair_width = q.shape
+    steps = fresh_k.shape[0]
+    group = QH // KVH
+    rows = 2 * steps * group
+    pairs = KVH // 2
     chunk = min(LANES * SPAN, seq_len)
     spans = chunk // SPAN
-    fine = tables[2].shape[0]
     total = pairs * rows
     whole = lambda *shape: vmem(shape, lambda i: (0,) * len(shape))
-    stat = jax.ShapeDtypeStruct((total, LANES), jnp.float32)
+    deal = (devices, 2 * steps * (QH // devices), LANES)
+    anywhere = pl.BlockSpec(memory_space=pl.ANY)
     return pl.pallas_call(
         attend_kernel,
         grid=(seq_len // chunk,),
-        out_shape=(jax.ShapeDtypeStruct((seq_len, rank), jnp.float32), stat, stat, stat),
+        out_shape=(
+            jax.ShapeDtypeStruct((rank, seq_len), jnp.float32),
+            jax.ShapeDtypeStruct(deal, jnp.float32),
+        ),
         in_specs=[
+            pl.BlockSpec(memory_space=pltpu.SMEM),
             vmem((chunk, width), lambda i: (i, 0)),
             vmem((chunk, width), lambda i: (i, 0)),
+            anywhere,
+            anywhere,
             whole(rank, width),
             whole(rank, width),
-            whole(pairs, rows, pair_width),
-            vmem((total, spans), lambda i: (0, i)),
-            vmem((chunk // fine, LANES), lambda i: (i, 0)),
-            vmem((chunk // fine, LANES), lambda i: (i, 0)),
-            whole(fine, LANES),
-            whole(fine, LANES),
-            whole(*xk.shape),
-            whole(*xv.shape),
-            whole(*xlive.shape),
+            whole(*q.shape),
+            vmem((live.shape[0], spans), lambda i: (0, i)),
+            whole(*cosine.shape),
+            whole(*sine.shape),
+            whole(*fresh_k.shape),
+            whole(*fresh_v.shape),
         ],
-        out_specs=(vmem((chunk, rank), lambda i: (i, 0)),) + (whole(total, LANES),) * 3,
+        out_specs=(vmem((rank, chunk), lambda i: (0, i)), whole(*deal)),
         scratch_shapes=[
-            pltpu.VMEM((pairs, 3 * rows, pair_width), jnp.bfloat16),
+            pltpu.VMEM((pairs, 3 * rows, 2 * HD), jnp.float32),
             pltpu.VMEM((spans, chunk), jnp.bfloat16),
+            pltpu.VMEM((total, live.shape[0]), jnp.bfloat16),
+            pltpu.VMEM((total, LANES), jnp.float32),
+            pltpu.VMEM((total, LANES), jnp.float32),
+            pltpu.VMEM((total, LANES), jnp.float32),
+            pltpu.VMEM((cosine.shape[0], LANES), jnp.float32),
+            pltpu.VMEM((cosine.shape[0], LANES), jnp.float32),
+            pltpu.VMEM((OMOST, SPAN, width), jnp.bfloat16),
+            pltpu.VMEM((OMOST, SPAN, width), jnp.bfloat16),
+            pltpu.VMEM((LANES, width), jnp.float32),
+            pltpu.VMEM((LANES, width), jnp.float32),
+            pltpu.SMEM((outliers.shape[0] + OMOST + 1,), jnp.int32),
+            pltpu.SemaphoreType.DMA((2, OMOST)),
         ],
         compiler_params=pltpu.CompilerParams(vmem_limit_bytes=VMEM_LIMIT),
         name="attend",
-    )(cache_keys, cache_values, basis, split, q, live, *tables, xk, xv, xlive)
+    )(
+        outliers, cache_keys, cache_values, cache_keys, cache_values, basis, split, q, live,
+        cosine, sine, fresh_k, fresh_v,
+    )
 
 
 def merge_kernel(devices, x_ref, out_ref, inbox, send_sem, recv_sem):
@@ -431,12 +563,6 @@
     return jnp.cos(angles), jnp.sin(angles)
 
 
-def rotate_halves(vectors, positions):
-    cosine, sine = waves(positions)
-    first, second = vectors[..., :HALF], vectors[..., HALF:]
-    return jnp.stack([first * cosine - second * sine, second * cosine + first * sine], axis=-2)
-
-
 def on_device(
     cache_keys,
     cache_values,
@@ -453,9 +579,7 @@
     myself = lax.axis_index("seq")
     length = seq_len * devices
     steps = queries.shape[0]
-    group = QH // KVH
     per_device = QH // devices
-    pairs = KVH // 2
     spans_dev = seq_len // SPAN
     base = myself * spans_dev
 
@@ -464,64 +588,24 @@
 
     own_spans = base + jnp.arange(spans_dev, dtype=jnp.int32)
     live = jnp.any(chosen[..., None] == own_spans, axis=2)
-    live = jnp.broadcast_to(
-        live.transpose(1, 0, 2)[:, :, None, :], (KVH, steps, group, spans_dev)
-    ).reshape(KVH * steps * group, spans_dev).astype(jnp.bfloat16)
-
-    outlier_here = outliers // spans_dev == myself
-    order = jnp.cumsum(outlier_here.astype(jnp.int32)) - 1
-    match = outlier_here & (order == jnp.arange(OMOST, dtype=jnp.int32)[:, None])
-    local = jnp.sum(jnp.where(match, outliers - base, 0), axis=1)
-    outlier_live = jnp.any(match, axis=1)
-    exact = [lax.dynamic_slice_in_dim(cache_keys, local[i] * SPAN, SPAN, 0) for i in range(OMOST)]
-    exact_v = [
-        lax.dynamic_slice_in_dim(cache_values, local[i] * SPAN, SPAN, 0) for i in range(OMOST)
-    ]
-    step_pos = length + jnp.arange(steps, dtype=jnp.int32)
-    token = jnp.arange(SPAN, dtype=jnp.int32)
-    extra_pos = jnp.concatenate([((local + base)[:, None] * SPAN + token).reshape(-1), step_pos])
-    count = OMOST * SPAN + steps
-    pad = ((0, LANES - count), (0, 0))
-    xk = jnp.concatenate(exact + [fresh_keys], axis=0).reshape(count, KVH, HD)
-    xk = rotate_halves(xk.astype(jnp.float32), extra_pos[:, None])
-    xk = xk.reshape(count, pairs, 2, 2, HALF).transpose(0, 1, 3, 2, 4).reshape(count, width)
-    xk = jnp.pad(xk.astype(jnp.bfloat16), pad)
-    xv = jnp.pad(jnp.concatenate(exact_v + [fresh_values], axis=0), pad)
-    causal = jnp.arange(steps)[None, :] <= jnp.arange(steps)[:, None]
-    extra_live = jnp.concatenate(
-        [
-            jnp.broadcast_to(jnp.repeat(outlier_live, SPAN), (steps, OMOST * SPAN)),
-            causal & (myself == 0),
-        ],
-        axis=1,
-    )
-    xlive = jnp.pad(extra_live.astype(jnp.float32), ((0, 0), (0, LANES - count)))
-    xlive = jnp.broadcast_to(
-        xlive[None, :, None, :], (KVH, steps, group, LANES)
-    ).reshape(KVH * steps * group, LANES)
-
-    score_scale = 1.0 / jnp.sqrt(jnp.float32(HD))
-    q = rotate_halves(queries.reshape(steps, QH, HD).astype(jnp.float32), step_pos[:, None])
-    q = (q * score_scale).reshape(steps, pairs, 2, group, 2, HALF).transpose(1, 2, 0, 3, 4, 5)
-    own_lane = jnp.eye(2, dtype=jnp.float32)[None, :, None, None, None, :, None]
-    q = (q[:, :, :, :, :, None, :] * own_lane).reshape(pairs, 2 * steps * group, 2 * HD)
-
-    fine = 64
-    coarse = jnp.arange(seq_len // fine, dtype=jnp.int32) * fine + myself * seq_len
-    tables = waves(coarse) + waves(jnp.arange(fine, dtype=jnp.int32))
-    tables = [jnp.concatenate([table, table], axis=1) for table in tables]
-
-    key_factor, out, top, total = attend(
-        cache_keys, cache_values, basis, split, q, live, tables, xk, xv, xlive
-    )
-
-    def deal(x):
-        x = x.reshape(KVH, steps, group // per_device, per_device, LANES)
-        return x.transpose(0, 2, 1, 3, 4).reshape(devices, steps * per_device, LANES)
-
-    stats = jnp.where(jnp.arange(LANES) < HALF, top, total)
-    attended = merge(jnp.concatenate([deal(out), deal(stats)], axis=1))
-    return (attended.reshape(steps, per_device * HD), key_factor)
+    live = live.reshape(steps * KVH, spans_dev).astype(jnp.bfloat16)
+    q = queries.astype(jnp.float32).reshape(steps * QH, HD) * (
+        1.0 / jnp.sqrt(jnp.float32(HD))
+    )
+    place = jnp.arange(seq_len // FINE + FINE + SPAN, dtype=jnp.int32)
+    coarse = seq_len // FINE
+    positions = jnp.where(
+        place < coarse,
+        place * FINE + myself * seq_len,
+        jnp.where(place < coarse + FINE, place - coarse, place - coarse - FINE + length),
+    )
+    cosine, sine = waves(positions)
+    factor_t, parts = attend(
+        cache_keys, cache_values, basis, split, q, live, cosine, sine, fresh_keys, fresh_values,
+        outliers, devices,
+    )
+    attended = merge(parts)
+    return (attended.reshape(steps, per_device * HD), factor_t.T)
 
 
 def solution(mesh):

time: 128 us -> 104 us (0.81)
  local copies, waits for them, and re-layouts: 18.9 us -> 2 us
  other arithmetic: 11 us -> 5.58 us
  between operations: 3.43 us -> 0.69 us
  Pallas kernels: 93.8 us -> 95.1 us
    unnamed x10 -> x0, local copies, waits for them, and re-layouts: 10.1 us -> none
    concatenate x4 -> x0, other arithmetic: 2.19 us -> none  [the longest x2 1.41 us: on_device(): tables = [jnp.concatenate([table, table], axis=1) for table in tables]]
    pad x2 -> x0, local copies, waits for them, and re-layouts: 1.47 us -> none  [the longest x1 0.74 us: on_device(): xk = jnp.pad(xk.astype(jnp.bfloat16), pad)]
    concatenate x3 -> x0, local copies, waits for them, and re-layouts: 1.42 us -> none  [the longest x1 0.71 us: on_device(): xv = jnp.pad(jnp.concatenate(exact_v + [fresh_values], axis=0), pad)]
    broadcast_in_dim x3 -> x0, local copies, waits for them, and re-layouts: 1.41 us -> none  [the longest x1 0.69 us: on_device(): jnp.broadcast_to(live.transpose(1, 0, 2)[:, :, None, :], (KVH, steps, gro...]
    pallas_call x1, Pallas kernels: 27.6 us -> 28.9 us  [attend(): pl.pallas_call(attend_kernel, grid=(seq_len // chunk,), out_shape=(jax.Sh...]
where the time goes in v2:
time: 104 us; the launch traced here: 103 us
  Pallas kernels  95.1 us (91%)
  other arithmetic  5.58 us (5%)
  local copies, waits for them, and re-layouts  2 us (2%)
    pallas_call x1, Pallas kernels, attend(): pl.pallas_call(attend_kernel, grid=(seq_len // chunk,), out_shape=(jax.Sh...  28.9 us
    pallas_call x1, Pallas kernels, sum_over_seq(): pl.pallas_call(functools.partial(sum_kernel, chips), out_shape=jax.ShapeD...  24.8 us
    pallas_call x1, Pallas kernels, make_basis(): pl.pallas_call(basis_kernel, out_shape=(shape, shape), in_specs=[vmem()],...  18.1 us
    pallas_call x1, Pallas kernels, merge(): pl.pallas_call(functools.partial(merge_kernel, devices), out_shape=jax.Sh...  12.3 us
    pallas_call x1, Pallas kernels, sketch_part(): pl.pallas_call(functools.partial(sketch_kernel, length), grid=(cache_keys...  11 us
    reduce_or x1, other arithmetic, on_device(): live = jnp.any(chosen[..., None] == own_spans, axis=2)  3.08 us

profile of v2, /device:TPU:0, one launch (start us, length us, event | category | flops | bytes accessed | tf_op | source)
XLA Modules:
  0.0 103.4 jit_solution(2445842366224224479)
XLA Ops:
  0.7 3.1 %compare_reduce_fusion = pred[3,8,512]{2,1,0:T(8,128)(4,1)S(1)} fusion(s32[512]{0:T(512)S(1)} %iota_add_fusion.2, s32[3,8,256]{2,1,0:T(8,128)} %param.15), kind=kLoop, calls=%fused_computation | loop fusion | flops 6279168 | bytes 38912 | tf_op jit(solution)/shard_map/reduce_or | solution.py:590
  3.8 0.6 convert_bitcast_fusion.live_ref
  4.4 0.9 convert_multiply_fusion
  5.3 0.7 mul.48.q_ref
  6.0 1.0 multiply_sine_fusion
  7.0 11.0 %sketch_part.1 = f32[160,8,128]{2,1,0:T(8,128)} custom-call(f32[160,1024]{1,0:T(8,128)} %bitcast.8, bf16[4096,1024]{1,0:T(8,128)(2,1)} %k_all.1), custom_call_target="tpu_custom_call" | custom-call | tf_op jit(solution)/shard_map/sketch_part/pallas_call | solution.py:76
  17.9 24.8 %sketch_sum.1 = f32[2,8,10,8,128]{4,3,2,1,0:T(8,128)} custom-call(f32[2,8,10,8,128]{4,3,2,1,0:T(8,128)} %bitcast.6), custom_call_target="tpu_custom_call" | custom-call | tf_op jit(solution)/shard_map/sketch_sum/pallas_call | solution.py:180
  42.8 18.1 %key_basis.1 = (bf16[160,1024]{1,0:T(8,128)(2,1)}, bf16[160,1024]{1,0:T(8,128)(2,1)}) custom-call(f32[160,8,128]{2,1,0:T(8,128)} %bitcast.7), custom_call_target="tpu_custom_call" | custom-call | tf_op jit(solution)/shard_map/key_basis/pallas_call | solution.py:251
  60.9 28.9 %attend.1 = (f32[160,4096]{1,0:T(8,128)}, f32[16,24,128]{2,1,0:T(8,128)}) custom-call(s32[32]{0:T(128)} %outl_ref.1, bf16[4096,1024]{1,0:T(8,128)(2,1)} %k_all.1, bf16[4096,1024]{1,0:T(8,128)(2,1)} %v_all.1, bf16[4096,1024]{1,0:T(8,128)(2,1)} %k_all.1, bf16[4096,1024]{1,0:T(8,128)(2,1)} %v_all.1, bf16[160,1024]{1,0:T(8,128)(2,1)} %get-tuple-element.6.basis_ref, ...), custom_call_target="tpu_custom_call" | custom-call | tf_op jit(solution)/shard_map/attend/pallas_call | solution.py:456
  89.8 12.3 %merge.1 = bf16[12,128]{1,0:T(8,128)(2,1)} custom-call(f32[16,24,128]{2,1,0:T(8,128)} %get-tuple-element.8.x_ref), custom_call_target="tpu_custom_call" | custom-call | tf_op jit(solution)/shard_map/merge/pallas_call | solution.py:544
  102.1 1.3 %reshape.48 = bf16[3,512]{1,0:T(4,128)(2,1)} reshape(bf16[12,128]{1,0:T(8,128)(2,1)} %merge.1) | data formatting | bytes 6144 | tf_op jit(solution)/shard_map/reshape | solution.py:608
  (3 shorter events, 0.0 us)
